TPU v7x, 256 devices: a whole 4x4x8 slice. The times are simulated.
256 devices in a mesh: group: 16 (over x_lo, y, core), dp: 16 (over x_hi, z).
Axes of the slice: x: 4 (x_hi: 2, x_lo: 2; x = x_hi * 2 + x_lo), y: 4, z: 8, core: 2. Of those that a mesh axis runs over, the one named last changes fastest.
Arguments:
- latents: bfloat16 [16, 512, 6144], P('group', 'dp'), may hold values from -6 to 6
- steps: int32 [16], P('group'), may hold values from 0 to 15
- segment_ids: int32 [512], replicated, may hold values from 0 to 15, never falling along the last dimension, each value on 1 to 64 neighbouring positions
- mod_table: float32 [16, 2, 6144], replicated, may hold values from -3 to 3
- w_query: bfloat16 [6144, 4096], P(None, 'dp')
- w_key: bfloat16 [6144, 4096], P(None, 'dp')
- w_value: bfloat16 [6144, 4096], P(None, 'dp'), may hold values from -0.3125 to 0.3125
Outputs:
- attended: bfloat16 [16, 512, 4096], P('group', 'dp')
Inputs may be any that keep to these rules, and one draw needn't show every extreme that they name: `segment_ids`: rows of one clip are contiguous; every clip index occurs, a clip holds 1 to 64 rows and one holds exactly that many.
All inputs are finite; a program needn't handle non-finite values.
Results may differ from a plain program's by a relative error of at most 0.011.
Values may be sent and summed in bfloat16 or wider, within the bound.
A program may use at most 128 MiB of HBM per device.

v0:
```python
import math
import jax
import jax.numpy as jnp
from jax import lax
from jax.sharding import PartitionSpec as P

D = 6144
HD = 128
HEAD_DEV = 2
STEPS = 16


def in_one_piece(arrays, axis, dim, along):
    both = jnp.concatenate(arrays, axis=along)
    out, at, gathered = (lax.all_gather(both, axis, axis=dim, tiled=True), 0, [])
    for a in arrays:
        gathered.append(lax.slice_in_dim(out, at, at + a.shape[along], axis=along))
        at += a.shape[along]
    return tuple(gathered)


def per_device(latents, steps, segment_ids, mod_table, w_query, w_key, w_value):
    rows_here = latents.shape[1]
    tokc = rows_here * lax.axis_size("dp")
    width = HEAD_DEV * HD
    x = latents[0].astype(jnp.float32)
    normed = x * lax.rsqrt(jnp.mean(x * x, axis=-1, keepdims=True) + 1e-06)
    picker = (steps[:, None] == jnp.arange(STEPS, dtype=jnp.int32)[None, :]).astype(jnp.float32)
    modulation = jnp.dot(picker, mod_table.reshape(STEPS, 2 * D), precision=lax.Precision.HIGHEST)
    modulated = (normed * (1.0 + modulation[:, :D]) + modulation[:, D:]).astype(jnp.bfloat16)
    piece = lax.all_gather(modulated, "dp", axis=0, tiled=True)
    first = jnp.dot(piece, w_query, preferred_element_type=jnp.float32).astype(jnp.bfloat16)
    second = jnp.dot(piece, w_key, preferred_element_type=jnp.float32).astype(jnp.bfloat16)
    third = jnp.dot(piece, w_value, preferred_element_type=jnp.float32).astype(jnp.bfloat16)
    projected = jnp.concatenate([first, second, third], axis=1)
    query = projected[:, :width].reshape(tokc, HEAD_DEV, HD)
    keys_own = projected[:, width : 2 * width]
    values_own = projected[:, 2 * width :]
    mine = lax.axis_index("group")
    same_clip = segment_ids[:, None] == segment_ids[None, :]
    inverse = 1.0 / math.sqrt(HD)

    def update(carry, key_block, value_block):
        best, total, accum = carry
        scores = (
            jnp.einsum(
                "thd,khd->htk",
                query,
                key_block.reshape(tokc, HEAD_DEV, HD),
                preferred_element_type=jnp.float32,
            )
            * inverse
        )
        scores = jnp.where(same_clip[None], scores, -1e30)
        new_best = jnp.maximum(best, jnp.max(scores, axis=-1))
        weights = jnp.where(same_clip[None], jnp.exp(scores - new_best[:, :, None]), 0.0)
        fade = jnp.exp(best - new_best)
        total = total * fade + jnp.sum(weights, axis=-1)
        added = jnp.einsum(
            "htk,khd->thd",
            weights.astype(jnp.bfloat16),
            value_block.reshape(tokc, HEAD_DEV, HD),
            preferred_element_type=jnp.float32,
        )
        accum = accum * jnp.transpose(fade)[:, :, None] + added
        return (new_best, total, accum)

    def visit(carry, key_block, value_block, source):
        usable = jnp.logical_and(source <= mine, source >= 0)
        return lax.cond(
            usable, lambda state: update(state, key_block, value_block), lambda state: state, carry
        )

    start_state = (
        jnp.full((HEAD_DEV, tokc), -1e30, jnp.float32),
        jnp.zeros((HEAD_DEV, tokc), jnp.float32),
        jnp.zeros((tokc, HEAD_DEV, HD), jnp.float32),
    )
    piece = in_one_piece((keys_own, values_own), "group", 0, 1)
    count = piece[0].shape[0] // tokc

    def single(index, state):
        key_block = lax.dynamic_slice_in_dim(piece[0], index * tokc, tokc, 0)
        value_block = lax.dynamic_slice_in_dim(piece[1], index * tokc, tokc, 0)
        return visit(state, key_block, value_block, index)

    carry = lax.fori_loop(0, count, single, start_state)
    best, total, accum = carry
    result = (accum / jnp.transpose(total)[:, :, None]).reshape(tokc, width).astype(jnp.bfloat16)
    regrouped = lax.all_to_all(result, "dp", split_axis=0, concat_axis=1, tiled=True)
    return regrouped[None]


def solution(mesh):
    placed = (
        P("group", "dp", None),
        P("group"),
        P(),
        P(),
        P(None, "dp"),
        P(None, "dp"),
        P(None, "dp"),
    )
    return jax.shard_map(
        per_device, mesh=mesh, in_specs=placed, out_specs=P("group", "dp", None), check_vma=False
    )
```

profile of v0, /device:TPU:27, one launch (start us, length us, event | category | flops | bytes accessed | tf_op | source)
XLA Modules:
  0.0 297.3 jit_solution(8042137725669814860)
XLA Ops:
  7.3 1.3 fusion.15
  8.7 1.6 copy.26
  11.7 116.8 %all-gather.3.cloned.1.call-done = bf16[512,6144]{1,0:T(8,128)(2,1)} async-done(((bf16[32,6144]{1,0:T(8,128)(2,1)}), bf16[512,6144]{1,0:T(8,128)(2,1)}) %all-gather.3.cloned.1.call-update) | async-done | bytes 6291472 | tf_op jit(solution)/shard_map/all_gather | solution.py:31
  128.5 4.8 %convolution_convert_fusion.1 = bf16[512,256]{0,1:T(8,128)(2,1)S(1)} fusion(bf16[512,6144]{1,0:T(8,128)(2,1)} %all-gather.3.cloned.1.call-done, bf16[6144,256]{1,0:T(8,128)(2,1)S(1)} %copy-done), kind=kOutput, calls=%fused_computation.22 | convolution fusion | flops 1610743808 | bytes 9699328 | tf_op jit(solution)/shard_map/dot_general | solution.py:34
  134.0 1.8 convolution_convert_fusion.2
  136.7 6.3 %convolution_convert_fusion = bf16[512,256]{0,1:T(8,128)(2,1)} fusion(bf16[512,6144]{1,0:T(8,128)(2,1)} %all-gather.3.cloned.1.call-done, bf16[6144,256]{1,0:T(8,128)(2,1)} %param.15), kind=kOutput, calls=%fused_computation.21 | convolution fusion | flops 1610743808 | bytes 9699328 | tf_op jit(solution)/shard_map/dot_general | solution.py:32
  144.1 45.9 %all-gather.5.cloned.1.call-done = bf16[8192,512]{0,1:T(8,128)(2,1)} async-done(((bf16[512,512]{0,1:T(8,128)(2,1)}), bf16[8192,512]{0,1:T(8,128)(2,1)}) %all-gather.5.cloned.1.call-update) | async-done | bytes 8388624 | tf_op jit(solution)/shard_map/all_gather | solution.py:15
  190.0 5.9 %fusion.24 = (bf16[8192,256]{0,1:T(8,128)(2,1)}, bf16[8192,256]{0,1:T(8,128)(2,1)}) fusion(bf16[8192,512]{0,1:T(8,128)(2,1)} %all-gather.5.cloned.1.call-done), kind=kLoop, calls=%fused_computation.39 | loop fusion | bytes 16777216 | tf_op jit(solution)/shard_map/slice | solution.py:17
  196.7 72.6 %while.18 = (s32[]{:T(128)}, f32[2,512]{1,0:T(2,128)S(1)}, f32[2,512]{1,0:T(2,128)S(1)}, f32[512,2,128]{2,0,1:T(8,128)}, s32[]{:T(128)}, /*index=5*/bf16[8192,25...) while((s32[]{:T(128)}, f32[2,512]{1,0:T(2,128)S(1)}, ...), condition=%wide.region_6.7_spmd.clone, body=%wide.region_1.6_spmd.clone.sunk | while | flops 275778560 | bytes 14487929 | solution.py:87
  196.7 4.5 %conditional.3 = ((f32[2,512]{1,0:T(2,128)S(1)}, f32[2,512]{1,0:T(2,128)S(1)}, f32[512,2,128]{2,0,1:T(8,128)})) conditional(s32[]{:T(128)} %convert_element_type.58, (f32[2,512]{1,0:T(2,128)S(1)}, f32[2,512]{1,0:T(2,128)S(1)}, f32[512,2,128]{2,0,1:T(8,128)}) %tuple.61, (s32[512]{0:T(512)S(1)}, s32[]{:T(128)}, bf16[8192,256]{0,1:T(8,128)(2,1)}, ...), branch_computations={%region_2.0_spmd, %region_3.5_spmd} | conditional | flops 275778560 | bytes 14487690 | solution.py:70
  196.9 1.1 constant_dynamic-slice_fusion
  201.2 4.5 %conditional.3 = ((f32[2,512]{1,0:T(2,128)S(1)}, f32[2,512]{1,0:T(2,128)S(1)}, f32[512,2,128]{2,0,1:T(8,128)})) conditional(s32[]{:T(128)} %convert_element_type.58, (f32[2,512]{1,0:T(2,128)S(1)}, f32[2,512]{1,0:T(2,128)S(1)}, f32[512,2,128]{2,0,1:T(8,128)}) %tuple.61, (s32[512]{0:T(512)S(1)}, s32[]{:T(128)}, bf16[8192,256]{0,1:T(8,128)(2,1)}, ...), branch_computations={%region_2.0_spmd, %region_3.5_spmd} | conditional | flops 275778560 | bytes 14487690 | solution.py:70
  205.7 4.5 %conditional.3 = ((f32[2,512]{1,0:T(2,128)S(1)}, f32[2,512]{1,0:T(2,128)S(1)}, f32[512,2,128]{2,0,1:T(8,128)})) conditional(s32[]{:T(128)} %convert_element_type.58, (f32[2,512]{1,0:T(2,128)S(1)}, f32[2,512]{1,0:T(2,128)S(1)}, f32[512,2,128]{2,0,1:T(8,128)}) %tuple.61, (s32[512]{0:T(512)S(1)}, s32[]{:T(128)}, bf16[8192,256]{0,1:T(8,128)(2,1)}, ...), branch_computations={%region_2.0_spmd, %region_3.5_spmd} | conditional | flops 275778560 | bytes 14487690 | solution.py:70
  206.0 1.1 constant_dynamic-slice_fusion
  210.3 4.5 %conditional.3 = ((f32[2,512]{1,0:T(2,128)S(1)}, f32[2,512]{1,0:T(2,128)S(1)}, f32[512,2,128]{2,0,1:T(8,128)})) conditional(s32[]{:T(128)} %convert_element_type.58, (f32[2,512]{1,0:T(2,128)S(1)}, f32[2,512]{1,0:T(2,128)S(1)}, f32[512,2,128]{2,0,1:T(8,128)}) %tuple.61, (s32[512]{0:T(512)S(1)}, s32[]{:T(128)}, bf16[8192,256]{0,1:T(8,128)(2,1)}, ...), branch_computations={%region_2.0_spmd, %region_3.5_spmd} | conditional | flops 275778560 | bytes 14487690 | solution.py:70
  210.5 1.1 constant_dynamic-slice_fusion
  214.8 4.5 %conditional.3 = ((f32[2,512]{1,0:T(2,128)S(1)}, f32[2,512]{1,0:T(2,128)S(1)}, f32[512,2,128]{2,0,1:T(8,128)})) conditional(s32[]{:T(128)} %convert_element_type.58, (f32[2,512]{1,0:T(2,128)S(1)}, f32[2,512]{1,0:T(2,128)S(1)}, f32[512,2,128]{2,0,1:T(8,128)}) %tuple.61, (s32[512]{0:T(512)S(1)}, s32[]{:T(128)}, bf16[8192,256]{0,1:T(8,128)(2,1)}, ...), branch_computations={%region_2.0_spmd, %region_3.5_spmd} | conditional | flops 275778560 | bytes 14487690 | solution.py:70
  219.4 4.5 %conditional.3 = ((f32[2,512]{1,0:T(2,128)S(1)}, f32[2,512]{1,0:T(2,128)S(1)}, f32[512,2,128]{2,0,1:T(8,128)})) conditional(s32[]{:T(128)} %convert_element_type.58, (f32[2,512]{1,0:T(2,128)S(1)}, f32[2,512]{1,0:T(2,128)S(1)}, f32[512,2,128]{2,0,1:T(8,128)}) %tuple.61, (s32[512]{0:T(512)S(1)}, s32[]{:T(128)}, bf16[8192,256]{0,1:T(8,128)(2,1)}, ...), branch_computations={%region_2.0_spmd, %region_3.5_spmd} | conditional | flops 275778560 | bytes 14487690 | solution.py:70
  219.6 1.1 constant_dynamic-slice_fusion
  223.9 4.5 %conditional.3 = ((f32[2,512]{1,0:T(2,128)S(1)}, f32[2,512]{1,0:T(2,128)S(1)}, f32[512,2,128]{2,0,1:T(8,128)})) conditional(s32[]{:T(128)} %convert_element_type.58, (f32[2,512]{1,0:T(2,128)S(1)}, f32[2,512]{1,0:T(2,128)S(1)}, f32[512,2,128]{2,0,1:T(8,128)}) %tuple.61, (s32[512]{0:T(512)S(1)}, s32[]{:T(128)}, bf16[8192,256]{0,1:T(8,128)(2,1)}, ...), branch_computations={%region_2.0_spmd, %region_3.5_spmd} | conditional | flops 275778560 | bytes 14487690 | solution.py:70
  224.2 1.1 constant_dynamic-slice_fusion
  228.4 4.5 %conditional.3 = ((f32[2,512]{1,0:T(2,128)S(1)}, f32[2,512]{1,0:T(2,128)S(1)}, f32[512,2,128]{2,0,1:T(8,128)})) conditional(s32[]{:T(128)} %convert_element_type.58, (f32[2,512]{1,0:T(2,128)S(1)}, f32[2,512]{1,0:T(2,128)S(1)}, f32[512,2,128]{2,0,1:T(8,128)}) %tuple.61, (s32[512]{0:T(512)S(1)}, s32[]{:T(128)}, bf16[8192,256]{0,1:T(8,128)(2,1)}, ...), branch_computations={%region_2.0_spmd, %region_3.5_spmd} | conditional | flops 275778560 | bytes 14487690 | solution.py:70
  233.0 4.5 %conditional.3 = ((f32[2,512]{1,0:T(2,128)S(1)}, f32[2,512]{1,0:T(2,128)S(1)}, f32[512,2,128]{2,0,1:T(8,128)})) conditional(s32[]{:T(128)} %convert_element_type.58, (f32[2,512]{1,0:T(2,128)S(1)}, f32[2,512]{1,0:T(2,128)S(1)}, f32[512,2,128]{2,0,1:T(8,128)}) %tuple.61, (s32[512]{0:T(512)S(1)}, s32[]{:T(128)}, bf16[8192,256]{0,1:T(8,128)(2,1)}, ...), branch_computations={%region_2.0_spmd, %region_3.5_spmd} | conditional | flops 275778560 | bytes 14487690 | solution.py:70
  237.5 4.5 %conditional.3 = ((f32[2,512]{1,0:T(2,128)S(1)}, f32[2,512]{1,0:T(2,128)S(1)}, f32[512,2,128]{2,0,1:T(8,128)})) conditional(s32[]{:T(128)} %convert_element_type.58, (f32[2,512]{1,0:T(2,128)S(1)}, f32[2,512]{1,0:T(2,128)S(1)}, f32[512,2,128]{2,0,1:T(8,128)}) %tuple.61, (s32[512]{0:T(512)S(1)}, s32[]{:T(128)}, bf16[8192,256]{0,1:T(8,128)(2,1)}, ...), branch_computations={%region_2.0_spmd, %region_3.5_spmd} | conditional | flops 275778560 | bytes 14487690 | solution.py:70
  242.1 4.5 %conditional.3 = ((f32[2,512]{1,0:T(2,128)S(1)}, f32[2,512]{1,0:T(2,128)S(1)}, f32[512,2,128]{2,0,1:T(8,128)})) conditional(s32[]{:T(128)} %convert_element_type.58, (f32[2,512]{1,0:T(2,128)S(1)}, f32[2,512]{1,0:T(2,128)S(1)}, f32[512,2,128]{2,0,1:T(8,128)}) %tuple.61, (s32[512]{0:T(512)S(1)}, s32[]{:T(128)}, bf16[8192,256]{0,1:T(8,128)(2,1)}, ...), branch_computations={%region_2.0_spmd, %region_3.5_spmd} | conditional | flops 275778560 | bytes 14487690 | solution.py:70
  246.6 4.5 %conditional.3 = ((f32[2,512]{1,0:T(2,128)S(1)}, f32[2,512]{1,0:T(2,128)S(1)}, f32[512,2,128]{2,0,1:T(8,128)})) conditional(s32[]{:T(128)} %convert_element_type.58, (f32[2,512]{1,0:T(2,128)S(1)}, f32[2,512]{1,0:T(2,128)S(1)}, f32[512,2,128]{2,0,1:T(8,128)}) %tuple.61, (s32[512]{0:T(512)S(1)}, s32[]{:T(128)}, bf16[8192,256]{0,1:T(8,128)(2,1)}, ...), branch_computations={%region_2.0_spmd, %region_3.5_spmd} | conditional | flops 275778560 | bytes 14487690 | solution.py:70
  251.1 4.5 %conditional.3 = ((f32[2,512]{1,0:T(2,128)S(1)}, f32[2,512]{1,0:T(2,128)S(1)}, f32[512,2,128]{2,0,1:T(8,128)})) conditional(s32[]{:T(128)} %convert_element_type.58, (f32[2,512]{1,0:T(2,128)S(1)}, f32[2,512]{1,0:T(2,128)S(1)}, f32[512,2,128]{2,0,1:T(8,128)}) %tuple.61, (s32[512]{0:T(512)S(1)}, s32[]{:T(128)}, bf16[8192,256]{0,1:T(8,128)(2,1)}, ...), branch_computations={%region_2.0_spmd, %region_3.5_spmd} | conditional | flops 275778560 | bytes 14487690 | solution.py:70
  255.7 4.5 %conditional.3 = ((f32[2,512]{1,0:T(2,128)S(1)}, f32[2,512]{1,0:T(2,128)S(1)}, f32[512,2,128]{2,0,1:T(8,128)})) conditional(s32[]{:T(128)} %convert_element_type.58, (f32[2,512]{1,0:T(2,128)S(1)}, f32[2,512]{1,0:T(2,128)S(1)}, f32[512,2,128]{2,0,1:T(8,128)}) %tuple.61, (s32[512]{0:T(512)S(1)}, s32[]{:T(128)}, bf16[8192,256]{0,1:T(8,128)(2,1)}, ...), branch_computations={%region_2.0_spmd, %region_3.5_spmd} | conditional | flops 275778560 | bytes 14487690 | solution.py:70
  260.2 4.5 %conditional.3 = ((f32[2,512]{1,0:T(2,128)S(1)}, f32[2,512]{1,0:T(2,128)S(1)}, f32[512,2,128]{2,0,1:T(8,128)})) conditional(s32[]{:T(128)} %convert_element_type.58, (f32[2,512]{1,0:T(2,128)S(1)}, f32[2,512]{1,0:T(2,128)S(1)}, f32[512,2,128]{2,0,1:T(8,128)}) %tuple.61, (s32[512]{0:T(512)S(1)}, s32[]{:T(128)}, bf16[8192,256]{0,1:T(8,128)(2,1)}, ...), branch_computations={%region_2.0_spmd, %region_3.5_spmd} | conditional | flops 275778560 | bytes 14487690 | solution.py:70
  264.7 4.5 %conditional.3 = ((f32[2,512]{1,0:T(2,128)S(1)}, f32[2,512]{1,0:T(2,128)S(1)}, f32[512,2,128]{2,0,1:T(8,128)})) conditional(s32[]{:T(128)} %convert_element_type.58, (f32[2,512]{1,0:T(2,128)S(1)}, f32[2,512]{1,0:T(2,128)S(1)}, f32[512,2,128]{2,0,1:T(8,128)}) %tuple.61, (s32[512]{0:T(512)S(1)}, s32[]{:T(128)}, bf16[8192,256]{0,1:T(8,128)(2,1)}, ...), branch_computations={%region_2.0_spmd, %region_3.5_spmd} | conditional | flops 275778560 | bytes 14487690 | solution.py:70
  269.3 1.2 divide_convert_fusion
  271.7 17.8 %all_to_all.13 = bf16[16,32,256]{2,1,0:T(8,128)(2,1)S(1)} all-to-all(bf16[16,32,256]{2,1,0:T(8,128)(2,1)} %convert_element_type.47), channel_id=1, replica_groups=mesh['group'=16,'dp'=16] {'dp'}, dimensions={0} | all-to-all | bytes 524288 | tf_op jit(solution)/shard_map/all_to_all | solution.py:90
  (214 shorter events, 72.2 us)
Async XLA Ops:
  6.5 121.9 %copy-start = (bf16[6144,256]{1,0:T(8,128)(2,1)S(1)}, bf16[6144,256]{1,0:T(8,128)(2,1)}, u32[]{:S(2)}) copy-start(bf16[6144,256]{1,0:T(8,128)(2,1)} %param.17) | copy-start | bytes 9437188
  6.5 4.1 %copy-start.3 = (bf16[1,32,6144]{2,1,0:T(8,128)(2,1)S(1)}, bf16[1,32,6144]{2,1,0:T(8,128)(2,1)}, u32[]{:S(2)}) copy-start(bf16[1,32,6144]{2,1,0:T(8,128)(2,1)} %param.11) | copy-start | bytes 1179652
  6.5 121.9 %all-gather.3.cloned.1.call-start = ((), (), s32[]{:S(2)}) async-start(), calls=%async_computation.1 | async-start | bytes 6684672 | tf_op jit(solution)/shard_map/all_gather | solution.py:31
  11.6 178.3 %all-gather.5.cloned.1.call-start = ((), (), s32[]{:S(2)}) async-start(), calls=%async_computation.2 | async-start | bytes 8912896 | tf_op jit(solution)/shard_map/all_gather | solution.py:15
  128.4 4.8 %copy-start.5 = (bf16[512,6144]{1,0:T(8,128)(2,1)S(1)}, bf16[512,6144]{1,0:T(8,128)(2,1)}, u32[]{:S(2)}) copy-start(bf16[512,6144]{1,0:T(8,128)(2,1)} %all-gather.3.cloned.1.call-done) | copy-start | bytes 18874372
  128.4 5.5 %copy-start.6 = (bf16[6144,256]{1,0:T(8,128)(2,1)S(1)}, bf16[6144,256]{1,0:T(8,128)(2,1)}, u32[]{:S(2)}) copy-start(bf16[6144,256]{1,0:T(8,128)(2,1)} %param.16) | copy-start | bytes 9437188
  144.0 52.6 %copy-start.4 = (s32[512]{0:T(512)S(1)}, s32[512]{0:T(512)}, u32[]{:S(2)}) copy-start(s32[512]{0:T(512)} %param.13) | copy-start | bytes 6148
  196.9 2.4 copy-start.1
  200.3 0.8 copy-start.2
  201.4 2.4 copy-start.1
  204.9 0.8 copy-start.2
  206.0 2.4 copy-start.1
  209.4 0.8 copy-start.2
  210.5 2.4 copy-start.1
  214.0 0.8 copy-start.2
  215.1 2.4 copy-start.1
  218.5 0.8 copy-start.2
  219.6 2.4 copy-start.1
  223.0 0.8 copy-start.2
  224.1 2.4 copy-start.1
  227.6 0.8 copy-start.2
  228.7 2.4 copy-start.1
  232.1 0.8 copy-start.2
  233.2 2.4 copy-start.1
  237.8 2.4 copy-start.1
  242.3 2.4 copy-start.1
  246.8 2.4 copy-start.1
  251.4 2.4 copy-start.1
  255.9 2.4 copy-start.1
  260.5 2.4 copy-start.1
  265.0 2.4 copy-start.1
  268.4 0.8 copy-start.2
  (7 other events, 5.6 us)
Sparse Core Ops, SparseCore 0:
  11.8 116.6 all-gather.2
  136.8 53.1 all-gather.4
where the time goes:
time: 298 us; the launch traced here: 297 us
  waiting for transfers between devices  163 us (55%)
  local copies, waits for them, and re-layouts  43.1 us (14%)
  matrix products  40.3 us (14%)
  blocking collectives  17.8 us (6%)
  other arithmetic  17.2 us (6%)
  between operations  14.3 us (5%)
    all_gather x1, waiting for transfers between devices, per_device(): piece = lax.all_gather(modulated, 'dp', axis=0, tiled=True)  117 us
    all_gather x1, waiting for transfers between devices, in_one_piece(): lax.all_gather(both, axis, axis=dim, tiled=True)  45.9 us
    dynamic_slice x16, local copies, waits for them, and re-layouts, single(): value_block = lax.dynamic_slice_in_dim(piece[1], index * tokc, tokc, 0)  18.1 us
    all_to_all x1, blocking collectives, per_device(): lax.all_to_all(result, 'dp', split_axis=0, concat_axis=1, tiled=True)  17.8 us
    dot_general x16, matrix products, update(): jnp.einsum('htk,khd->thd', weights.astype(jnp.bfloat16), value_block.resh...  17 us
    cond x80, local copies, waits for them, and re-layouts  12.7 us
    dot_general x16, matrix products, update(): jnp.einsum('thd,khd->htk', query, key_block.reshape(tokc, HEAD_DEV, HD),...  10.1 us
    reduce_sum x16, other arithmetic, update(): total = total * fade + jnp.sum(weights, axis=-1)  9.03 us
  transfers between devices with their start and end apart: 2, of which 2 were waited for; matrix products, arithmetic and copies ran while one was open for 2% of the time, Pallas kernels for 0%

commit v1 on v0

--- a/solution.py
+++ b/solution.py
@@ -28,7 +28,9 @@
     picker = (steps[:, None] == jnp.arange(STEPS, dtype=jnp.int32)[None, :]).astype(jnp.float32)
     modulation = jnp.dot(picker, mod_table.reshape(STEPS, 2 * D), precision=lax.Precision.HIGHEST)
     modulated = (normed * (1.0 + modulation[:, :D]) + modulation[:, D:]).astype(jnp.bfloat16)
-    piece = lax.all_gather(modulated, "dp", axis=0, tiled=True)
+    piece = jnp.concatenate(
+        lax.all_to_all(jnp.stack([modulated] * lax.axis_size("dp")), "dp", 0, 0), axis=0
+    )
     first = jnp.dot(piece, w_query, preferred_element_type=jnp.float32).astype(jnp.bfloat16)
     second = jnp.dot(piece, w_key, preferred_element_type=jnp.float32).astype(jnp.bfloat16)
     third = jnp.dot(piece, w_value, preferred_element_type=jnp.float32).astype(jnp.bfloat16)

time: 298 us -> 330 us (1.11)
  blocking collectives: 17.8 us -> 166 us
  waiting for transfers between devices: 163 us -> 46.5 us
    all_to_all x0 -> x1, blocking collectives: none -> 148 us  [per_device(): lax.all_to_all(jnp.stack([modulated] * lax.axis_size('dp')), 'dp', 0, 0)]
    all_gather x1 -> x0, waiting for transfers between devices: 117 us -> none  [per_device(): piece = lax.all_gather(modulated, 'dp', axis=0, tiled=True)]
  transfers between devices with their start and end apart: 2 -> 1, of which waited for: 2 -> 1; matrix products, arithmetic and copies ran while one was open for 2% -> 2% of each run, Pallas kernels for 0% -> 0%
where the time goes in v1:
time: 330 us; the launch traced here: 329 us
  blocking collectives  166 us (50%)
  waiting for transfers between devices  46.5 us (14%)
  local copies, waits for them, and re-layouts  46.3 us (14%)
  matrix products  37.4 us (11%)
  other arithmetic  16.5 us (5%)
  between operations  14.3 us (4%)
    all_to_all x1, blocking collectives, per_device(): lax.all_to_all(jnp.stack([modulated] * lax.axis_size('dp')), 'dp', 0, 0)  148 us
    all_gather x1, waiting for transfers between devices, in_one_piece(): lax.all_gather(both, axis, axis=dim, tiled=True)  46.5 us
    dynamic_slice x16, local copies, waits for them, and re-layouts, single(): value_block = lax.dynamic_slice_in_dim(piece[1], index * tokc, tokc, 0)  18.1 us
    all_to_all x1, blocking collectives, per_device(): lax.all_to_all(result, 'dp', split_axis=0, concat_axis=1, tiled=True)  17.6 us
    dot_general x16, matrix products, update(): jnp.einsum('htk,khd->thd', weights.astype(jnp.bfloat16), value_block.resh...  17 us
    cond x80, local copies, waits for them, and re-layouts  12.7 us
    dot_general x16, matrix products, update(): jnp.einsum('thd,khd->htk', query, key_block.reshape(tokc, HEAD_DEV, HD),...  10.1 us
    reduce_sum x16, other arithmetic, update(): total = total * fade + jnp.sum(weights, axis=-1)  9.03 us
  transfers between devices with their start and end apart: 1, of which 1 were waited for; matrix products, arithmetic and copies ran while one was open for 2% of the time, Pallas kernels for 0%

profile of v1, /device:TPU:27, one launch (start us, length us, event | category | flops | bytes accessed | tf_op | source)
XLA Modules:
  0.0 328.9 jit_solution(1734220689917225127)
XLA Ops:
  7.3 1.3 fusion.15
  8.7 1.6 copy.26
  11.6 148.5 %all_to_all.18 = bf16[16,32,6144]{2,1,0:T(8,128)(2,1)S(1)} all-to-all(bf16[16,32,6144]{2,1,0:T(8,128)(2,1)S(1)} %stack.5), channel_id=1, replica_groups=mesh['group'=16,'dp'=16] {'dp'}, dimensions={0} | all-to-all | bytes 12582912 | tf_op jit(solution)/shard_map/all_to_all | solution.py:32
  160.1 1.9 convolution_convert_fusion.1
  162.0 1.3 copy-done.1
  164.3 1.8 convolution_convert_fusion.2
  167.0 6.3 %convolution_convert_fusion = bf16[512,256]{0,1:T(8,128)(2,1)} fusion(bf16[512,6144]{1,0:T(8,128)(2,1)} %bitcast.50, bf16[6144,256]{1,0:T(8,128)(2,1)} %param.15), kind=kOutput, calls=%fused_computation.21 | convolution fusion | flops 1610743808 | bytes 9699328 | tf_op jit(solution)/shard_map/dot_general | solution.py:34
  174.4 46.5 %all-gather.2.cloned.1.call-done = bf16[8192,512]{0,1:T(8,128)(2,1)} async-done(((bf16[512,512]{0,1:T(8,128)(2,1)}), bf16[8192,512]{0,1:T(8,128)(2,1)}) %all-gather.2.cloned.1.call-update) | async-done | bytes 8388624 | tf_op jit(solution)/shard_map/all_gather | solution.py:15
  220.9 5.9 %fusion.25 = (bf16[8192,256]{0,1:T(8,128)(2,1)}, bf16[8192,256]{0,1:T(8,128)(2,1)}) fusion(bf16[8192,512]{0,1:T(8,128)(2,1)} %all-gather.2.cloned.1.call-done), kind=kLoop, calls=%fused_computation.40 | loop fusion | bytes 16777216 | tf_op jit(solution)/shard_map/slice | solution.py:17
  227.6 72.5 %while.18 = (s32[]{:T(128)}, f32[2,512]{1,0:T(2,128)S(1)}, f32[2,512]{1,0:T(2,128)S(1)}, f32[512,2,128]{2,0,1:T(8,128)}, s32[]{:T(128)}, /*index=5*/bf16[8192,25...) while((s32[]{:T(128)}, f32[2,512]{1,0:T(2,128)S(1)}, ...), condition=%wide.region_6.7_spmd.clone, body=%wide.region_1.6_spmd.clone.sunk | while | flops 275778560 | bytes 14487929 | solution.py:89
  227.6 4.5 %conditional.3 = ((f32[2,512]{1,0:T(2,128)S(1)}, f32[2,512]{1,0:T(2,128)S(1)}, f32[512,2,128]{2,0,1:T(8,128)})) conditional(s32[]{:T(128)} %convert_element_type.70, (f32[2,512]{1,0:T(2,128)S(1)}, f32[2,512]{1,0:T(2,128)S(1)}, f32[512,2,128]{2,0,1:T(8,128)}) %tuple.61, (s32[512]{0:T(512)S(1)}, s32[]{:T(128)}, bf16[8192,256]{0,1:T(8,128)(2,1)}, ...), branch_computations={%region_2.0_spmd, %region_3.5_spmd} | conditional | flops 275778560 | bytes 14487690 | solution.py:72
  227.8 1.1 constant_dynamic-slice_fusion
  232.1 4.5 %conditional.3 = ((f32[2,512]{1,0:T(2,128)S(1)}, f32[2,512]{1,0:T(2,128)S(1)}, f32[512,2,128]{2,0,1:T(8,128)})) conditional(s32[]{:T(128)} %convert_element_type.70, (f32[2,512]{1,0:T(2,128)S(1)}, f32[2,512]{1,0:T(2,128)S(1)}, f32[512,2,128]{2,0,1:T(8,128)}) %tuple.61, (s32[512]{0:T(512)S(1)}, s32[]{:T(128)}, bf16[8192,256]{0,1:T(8,128)(2,1)}, ...), branch_computations={%region_2.0_spmd, %region_3.5_spmd} | conditional | flops 275778560 | bytes 14487690 | solution.py:72
  236.7 4.5 %conditional.3 = ((f32[2,512]{1,0:T(2,128)S(1)}, f32[2,512]{1,0:T(2,128)S(1)}, f32[512,2,128]{2,0,1:T(8,128)})) conditional(s32[]{:T(128)} %convert_element_type.70, (f32[2,512]{1,0:T(2,128)S(1)}, f32[2,512]{1,0:T(2,128)S(1)}, f32[512,2,128]{2,0,1:T(8,128)}) %tuple.61, (s32[512]{0:T(512)S(1)}, s32[]{:T(128)}, bf16[8192,256]{0,1:T(8,128)(2,1)}, ...), branch_computations={%region_2.0_spmd, %region_3.5_spmd} | conditional | flops 275778560 | bytes 14487690 | solution.py:72
  236.9 1.1 constant_dynamic-slice_fusion
  241.2 4.5 %conditional.3 = ((f32[2,512]{1,0:T(2,128)S(1)}, f32[2,512]{1,0:T(2,128)S(1)}, f32[512,2,128]{2,0,1:T(8,128)})) conditional(s32[]{:T(128)} %convert_element_type.70, (f32[2,512]{1,0:T(2,128)S(1)}, f32[2,512]{1,0:T(2,128)S(1)}, f32[512,2,128]{2,0,1:T(8,128)}) %tuple.61, (s32[512]{0:T(512)S(1)}, s32[]{:T(128)}, bf16[8192,256]{0,1:T(8,128)(2,1)}, ...), branch_computations={%region_2.0_spmd, %region_3.5_spmd} | conditional | flops 275778560 | bytes 14487690 | solution.py:72
  241.4 1.1 constant_dynamic-slice_fusion
  245.7 4.5 %conditional.3 = ((f32[2,512]{1,0:T(2,128)S(1)}, f32[2,512]{1,0:T(2,128)S(1)}, f32[512,2,128]{2,0,1:T(8,128)})) conditional(s32[]{:T(128)} %convert_element_type.70, (f32[2,512]{1,0:T(2,128)S(1)}, f32[2,512]{1,0:T(2,128)S(1)}, f32[512,2,128]{2,0,1:T(8,128)}) %tuple.61, (s32[512]{0:T(512)S(1)}, s32[]{:T(128)}, bf16[8192,256]{0,1:T(8,128)(2,1)}, ...), branch_computations={%region_2.0_spmd, %region_3.5_spmd} | conditional | flops 275778560 | bytes 14487690 | solution.py:72
  246.0 1.1 constant_dynamic-slice_fusion
  250.3 4.5 %conditional.3 = ((f32[2,512]{1,0:T(2,128)S(1)}, f32[2,512]{1,0:T(2,128)S(1)}, f32[512,2,128]{2,0,1:T(8,128)})) conditional(s32[]{:T(128)} %convert_element_type.70, (f32[2,512]{1,0:T(2,128)S(1)}, f32[2,512]{1,0:T(2,128)S(1)}, f32[512,2,128]{2,0,1:T(8,128)}) %tuple.61, (s32[512]{0:T(512)S(1)}, s32[]{:T(128)}, bf16[8192,256]{0,1:T(8,128)(2,1)}, ...), branch_computations={%region_2.0_spmd, %region_3.5_spmd} | conditional | flops 275778560 | bytes 14487690 | solution.py:72
  254.8 4.5 %conditional.3 = ((f32[2,512]{1,0:T(2,128)S(1)}, f32[2,512]{1,0:T(2,128)S(1)}, f32[512,2,128]{2,0,1:T(8,128)})) conditional(s32[]{:T(128)} %convert_element_type.70, (f32[2,512]{1,0:T(2,128)S(1)}, f32[2,512]{1,0:T(2,128)S(1)}, f32[512,2,128]{2,0,1:T(8,128)}) %tuple.61, (s32[512]{0:T(512)S(1)}, s32[]{:T(128)}, bf16[8192,256]{0,1:T(8,128)(2,1)}, ...), branch_computations={%region_2.0_spmd, %region_3.5_spmd} | conditional | flops 275778560 | bytes 14487690 | solution.py:72
  259.3 4.5 %conditional.3 = ((f32[2,512]{1,0:T(2,128)S(1)}, f32[2,512]{1,0:T(2,128)S(1)}, f32[512,2,128]{2,0,1:T(8,128)})) conditional(s32[]{:T(128)} %convert_element_type.70, (f32[2,512]{1,0:T(2,128)S(1)}, f32[2,512]{1,0:T(2,128)S(1)}, f32[512,2,128]{2,0,1:T(8,128)}) %tuple.61, (s32[512]{0:T(512)S(1)}, s32[]{:T(128)}, bf16[8192,256]{0,1:T(8,128)(2,1)}, ...), branch_computations={%region_2.0_spmd, %region_3.5_spmd} | conditional | flops 275778560 | bytes 14487690 | solution.py:72
  263.9 4.5 %conditional.3 = ((f32[2,512]{1,0:T(2,128)S(1)}, f32[2,512]{1,0:T(2,128)S(1)}, f32[512,2,128]{2,0,1:T(8,128)})) conditional(s32[]{:T(128)} %convert_element_type.70, (f32[2,512]{1,0:T(2,128)S(1)}, f32[2,512]{1,0:T(2,128)S(1)}, f32[512,2,128]{2,0,1:T(8,128)}) %tuple.61, (s32[512]{0:T(512)S(1)}, s32[]{:T(128)}, bf16[8192,256]{0,1:T(8,128)(2,1)}, ...), branch_computations={%region_2.0_spmd, %region_3.5_spmd} | conditional | flops 275778560 | bytes 14487690 | solution.py:72
  268.4 4.5 %conditional.3 = ((f32[2,512]{1,0:T(2,128)S(1)}, f32[2,512]{1,0:T(2,128)S(1)}, f32[512,2,128]{2,0,1:T(8,128)})) conditional(s32[]{:T(128)} %convert_element_type.70, (f32[2,512]{1,0:T(2,128)S(1)}, f32[2,512]{1,0:T(2,128)S(1)}, f32[512,2,128]{2,0,1:T(8,128)}) %tuple.61, (s32[512]{0:T(512)S(1)}, s32[]{:T(128)}, bf16[8192,256]{0,1:T(8,128)(2,1)}, ...), branch_computations={%region_2.0_spmd, %region_3.5_spmd} | conditional | flops 275778560 | bytes 14487690 | solution.py:72
  272.9 4.5 %conditional.3 = ((f32[2,512]{1,0:T(2,128)S(1)}, f32[2,512]{1,0:T(2,128)S(1)}, f32[512,2,128]{2,0,1:T(8,128)})) conditional(s32[]{:T(128)} %convert_element_type.70, (f32[2,512]{1,0:T(2,128)S(1)}, f32[2,512]{1,0:T(2,128)S(1)}, f32[512,2,128]{2,0,1:T(8,128)}) %tuple.61, (s32[512]{0:T(512)S(1)}, s32[]{:T(128)}, bf16[8192,256]{0,1:T(8,128)(2,1)}, ...), branch_computations={%region_2.0_spmd, %region_3.5_spmd} | conditional | flops 275778560 | bytes 14487690 | solution.py:72
  277.5 4.5 %conditional.3 = ((f32[2,512]{1,0:T(2,128)S(1)}, f32[2,512]{1,0:T(2,128)S(1)}, f32[512,2,128]{2,0,1:T(8,128)})) conditional(s32[]{:T(128)} %convert_element_type.70, (f32[2,512]{1,0:T(2,128)S(1)}, f32[2,512]{1,0:T(2,128)S(1)}, f32[512,2,128]{2,0,1:T(8,128)}) %tuple.61, (s32[512]{0:T(512)S(1)}, s32[]{:T(128)}, bf16[8192,256]{0,1:T(8,128)(2,1)}, ...), branch_computations={%region_2.0_spmd, %region_3.5_spmd} | conditional | flops 275778560 | bytes 14487690 | solution.py:72
  282.0 4.5 %conditional.3 = ((f32[2,512]{1,0:T(2,128)S(1)}, f32[2,512]{1,0:T(2,128)S(1)}, f32[512,2,128]{2,0,1:T(8,128)})) conditional(s32[]{:T(128)} %convert_element_type.70, (f32[2,512]{1,0:T(2,128)S(1)}, f32[2,512]{1,0:T(2,128)S(1)}, f32[512,2,128]{2,0,1:T(8,128)}) %tuple.61, (s32[512]{0:T(512)S(1)}, s32[]{:T(128)}, bf16[8192,256]{0,1:T(8,128)(2,1)}, ...), branch_computations={%region_2.0_spmd, %region_3.5_spmd} | conditional | flops 275778560 | bytes 14487690 | solution.py:72
  286.6 4.5 %conditional.3 = ((f32[2,512]{1,0:T(2,128)S(1)}, f32[2,512]{1,0:T(2,128)S(1)}, f32[512,2,128]{2,0,1:T(8,128)})) conditional(s32[]{:T(128)} %convert_element_type.70, (f32[2,512]{1,0:T(2,128)S(1)}, f32[2,512]{1,0:T(2,128)S(1)}, f32[512,2,128]{2,0,1:T(8,128)}) %tuple.61, (s32[512]{0:T(512)S(1)}, s32[]{:T(128)}, bf16[8192,256]{0,1:T(8,128)(2,1)}, ...), branch_computations={%region_2.0_spmd, %region_3.5_spmd} | conditional | flops 275778560 | bytes 14487690 | solution.py:72
  291.1 4.5 %conditional.3 = ((f32[2,512]{1,0:T(2,128)S(1)}, f32[2,512]{1,0:T(2,128)S(1)}, f32[512,2,128]{2,0,1:T(8,128)})) conditional(s32[]{:T(128)} %convert_element_type.70, (f32[2,512]{1,0:T(2,128)S(1)}, f32[2,512]{1,0:T(2,128)S(1)}, f32[512,2,128]{2,0,1:T(8,128)}) %tuple.61, (s32[512]{0:T(512)S(1)}, s32[]{:T(128)}, bf16[8192,256]{0,1:T(8,128)(2,1)}, ...), branch_computations={%region_2.0_spmd, %region_3.5_spmd} | conditional | flops 275778560 | bytes 14487690 | solution.py:72
  295.6 4.5 %conditional.3 = ((f32[2,512]{1,0:T(2,128)S(1)}, f32[2,512]{1,0:T(2,128)S(1)}, f32[512,2,128]{2,0,1:T(8,128)})) conditional(s32[]{:T(128)} %convert_element_type.70, (f32[2,512]{1,0:T(2,128)S(1)}, f32[2,512]{1,0:T(2,128)S(1)}, f32[512,2,128]{2,0,1:T(8,128)}) %tuple.61, (s32[512]{0:T(512)S(1)}, s32[]{:T(128)}, bf16[8192,256]{0,1:T(8,128)(2,1)}, ...), branch_computations={%region_2.0_spmd, %region_3.5_spmd} | conditional | flops 275778560 | bytes 14487690 | solution.py:72
  300.2 1.2 divide_convert_fusion
  303.5 17.6 %all_to_all.19 = bf16[16,32,256]{2,1,0:T(8,128)(2,1)S(1)} all-to-all(bf16[16,32,256]{2,1,0:T(8,128)(2,1)S(1)} %convert_element_type.46), channel_id=1, replica_groups=mesh['group'=16,'dp'=16] {'dp'}, dimensions={0} | all-to-all | bytes 524288 | tf_op jit(solution)/shard_map/all_to_all | solution.py:92
  (213 shorter events, 74.5 us)
Async XLA Ops:
  6.5 153.6 %copy-start = (bf16[6144,256]{1,0:T(8,128)(2,1)S(1)}, bf16[6144,256]{1,0:T(8,128)(2,1)}, u32[]{:S(2)}) copy-start(bf16[6144,256]{1,0:T(8,128)(2,1)} %param.17) | copy-start | bytes 9437188
  6.5 214.4 %all-gather.2.cloned.1.call-start = ((), (), s32[]{:S(2)}) async-start(), calls=%async_computation.2 | async-start | bytes 8912896 | tf_op jit(solution)/shard_map/all_gather | solution.py:15
  6.5 4.1 %copy-start.4 = (bf16[1,32,6144]{2,1,0:T(8,128)(2,1)S(1)}, bf16[1,32,6144]{2,1,0:T(8,128)(2,1)}, u32[]{:S(2)}) copy-start(bf16[1,32,6144]{2,1,0:T(8,128)(2,1)} %param.11) | copy-start | bytes 1179652
  160.1 3.2 copy-start.1
  160.1 4.2 %copy-start.6 = (bf16[6144,256]{1,0:T(8,128)(2,1)S(1)}, bf16[6144,256]{1,0:T(8,128)(2,1)}, u32[]{:S(2)}) copy-start(bf16[6144,256]{1,0:T(8,128)(2,1)} %param.16) | copy-start | bytes 9437188
  174.4 53.2 %copy-start.5 = (s32[512]{0:T(512)S(1)}, s32[512]{0:T(512)}, u32[]{:S(2)}) copy-start(s32[512]{0:T(512)} %param.13) | copy-start | bytes 6148
  227.8 2.4 copy-start.2
  231.3 0.8 copy-start.3
  232.4 2.4 copy-start.2
  235.8 0.8 copy-start.3
  236.9 2.4 copy-start.2
  240.3 0.8 copy-start.3
  241.4 2.4 copy-start.2
  244.9 0.8 copy-start.3
  246.0 2.4 copy-start.2
  249.4 0.8 copy-start.3
  250.5 2.4 copy-start.2
  254.0 0.8 copy-start.3
  255.0 2.4 copy-start.2
  258.5 0.8 copy-start.3
  259.6 2.4 copy-start.2
  263.0 0.8 copy-start.3
  264.1 2.4 copy-start.2
  268.7 2.4 copy-start.2
  272.1 0.8 copy-start.3
  273.2 2.4 copy-start.2
  276.6 0.8 copy-start.3
  277.7 2.4 copy-start.2
  282.3 2.4 copy-start.2
  286.8 2.4 copy-start.2
  291.3 2.4 copy-start.2
  295.9 2.4 copy-start.2
  (6 other events, 4.8 us)
Sparse Core Ops, SparseCore 0:
  167.1 53.7 all-gather.1
